TPU v7x, 256 devices: a whole 4x4x8 slice. The times are simulated.
256 devices in a mesh: samples: 256 (over y, z, x, core).
Axes of the slice: x: 4, y: 4, z: 8, core: 2. Of those that a mesh axis runs over, the one named last changes fastest.
Arguments:
- spin_configs: int32 [256, 256], P('samples'), may hold values from -1 to 1, as said below
- energy: float32 [256], P('samples'), may hold values from -6 to 6
- embedding: float32 [9, 64], replicated, may hold values from -2 to 2
- kernels: float32 [24, 9, 64, 64], replicated, may hold values from -0.25 to 0.25
- readout: float32 [64], replicated, may hold values from -0.75 to 0.75
Outputs:
- update_step: float32 [884736], P('samples')
Inputs may be any that keep to these rules, and one draw needn't show every extreme that they name: `spin_configs`: every entry is +1 or -1, and each sample has as many +1 as -1 entries.
All inputs are finite; a program needn't handle non-finite values.
Results may differ from a plain program's by a relative error of at most 0.004.
The roundings to bfloat16 on the way count: a program that leaves them out, or rounds other values in their place, can miss the bound.
Values may be sent and summed in bfloat16 or wider, within the bound.
No kernel may reach another device: no remote copies, remote signals or barrier semaphores. Data moves between devices by JAX's collectives and lax.ppermute only.
A program may use at most 128 MiB of HBM per device.

v0:
```python
import math

import jax
import jax.numpy as jnp
from jax import lax
from jax.sharding import PartitionSpec as P

SIDE = 16


shift_ratio = 0.05


def shifted_copies(values, lattice_side):
    channels = values.shape[0]
    lattice = values.reshape(channels, lattice_side, lattice_side)
    copies = [
        jnp.roll(lattice, (row_step, col_step), axis=(1, 2))
        for row_step in (1, 0, -1)
        for col_step in (1, 0, -1)
    ]
    return jnp.stack(copies, 0).reshape(9, channels, lattice_side * lattice_side)


def layer_norm(values):
    deviation = values - jnp.mean(values, axis=0, keepdims=True)
    return deviation * lax.rsqrt(jnp.mean(deviation * deviation, axis=0, keepdims=True) + 1e-05)


def block_step(hidden, kernel, lattice_side):
    active = jax.nn.gelu(layer_norm(hidden))
    return hidden + jnp.einsum(
        "kis,kio->os", shifted_copies(active, lattice_side), kernel, precision=lax.Precision.HIGHEST
    )


def log_amplitude(all_kernels, spin_row, embedding, readout, lattice_side):
    spin_field = spin_row.astype(jnp.float32)[None, :]
    hidden = jnp.einsum(
        "kcs,kcd->ds",
        shifted_copies(spin_field, lattice_side),
        embedding[:, None, :],
        precision=lax.Precision.HIGHEST,
    )
    hidden, unused = lax.scan(
        lambda carry, kernel: (block_step(carry, kernel, lattice_side), None), hidden, all_kernels
    )
    return jnp.sum(readout[:, None] * jax.nn.gelu(layer_norm(hidden))) / lattice_side


def solve_coeffs(gram_matrix, energy_all):
    sample_count = gram_matrix.shape[0]
    spread = (energy_all - jnp.mean(energy_all)) / math.sqrt(sample_count)
    diag_term = shift_ratio * jnp.mean(jnp.diagonal(gram_matrix)) + 1e-06
    system = gram_matrix + diag_term * jnp.eye(sample_count, dtype=jnp.float32)
    factor = jnp.linalg.cholesky(system)
    return jax.scipy.linalg.cho_solve((factor, True), spread)


def per_device(spin_configs, energy, embedding, kernels, readout):
    samples_here = spin_configs.shape[0]
    gradient = jax.grad(
        lambda all_kernels, spin_row: log_amplitude(all_kernels, spin_row, embedding, readout, SIDE)
    )
    logderiv = jax.vmap(gradient, in_axes=(None, 0))(kernels, spin_configs).reshape(
        samples_here, -1
    )
    full_len = logderiv.shape[1]
    sample_count = samples_here * lax.axis_size("samples")
    grad_total = lax.psum(jnp.sum(logderiv, axis=0), "samples")
    mean_row = grad_total / sample_count
    centered = ((logderiv - mean_row) / math.sqrt(sample_count)).astype(jnp.bfloat16)
    columns = lax.all_to_all(centered, "samples", split_axis=1, concat_axis=0, tiled=True)
    partial_gram = lax.dot_general(
        columns, columns, (((1,), (1,)), ((), ())), preferred_element_type=jnp.float32
    )
    gram_matrix = lax.psum(partial_gram, "samples")
    energy_all = lax.all_gather(energy, "samples", axis=0, tiled=True)
    coeffs = solve_coeffs(gram_matrix, energy_all)
    own_part = jnp.dot(coeffs, columns.astype(jnp.float32), precision=lax.Precision.HIGHEST)
    square_total = lax.psum(jnp.sum(own_part * own_part), "samples")
    return own_part * lax.rsqrt(square_total / full_len + 1e-06)


def solution(mesh):
    return jax.shard_map(
        per_device,
        mesh=mesh,
        in_specs=(P("samples", None), P("samples"), P(), P(), P()),
        out_specs=P("samples"),
        check_vma=False,
    )
```

profile of v0, /device:TPU:1, one launch (start us, length us, event | category | flops | bytes accessed | tf_op | source)
XLA Modules:
  0.0 1202.7 jit_solution(16037261148835651161)
XLA Ops:
  9.8 134.3 %while.43 = (s32[]{:T(128)}, f32[1,64,256]{2,1,0:T(8,128)S(1)}, f32[24,1,64,256]{3,2,1,0:T(8,128)}, f32[24,1,1,256]{3,2,1,0:T(1,128)S(1)}, f32[24,1,1,256]{3,2,1...) while((s32[]{:T(128)}, f32[1,64,256]{2,1,0:T(8,128)S(1)}, ...), condition=%wide.region_3.4_spmd, body=%wide.region_0.3_spmd.sunk | while | flops 114213632 | bytes 9556613 | solution.py:45
  144.6 3.7 broadcast_in_dim.88
  148.3 228.3 %while.44 = (s32[]{:T(128)}, f32[1,64,256]{1,2,0:T(8,128)S(1)}, f32[24,1,9,64,64]{4,3,2,1,0:T(8,128)}, f32[24,9,64,64]{3,2,1,0:T(8,128)}, f32[24,1,64,256]{3,2,1...) while((s32[]{:T(128)}, f32[1,64,256]{1,2,0:T(8,128)S(1)}, ...), condition=%wide.region_11.12_spmd, body=%wide.region_8.11_spmd.sunk | while | flops 227329024 | bytes 7526585 | solution.py:45
  155.2 2.4 fusion.151
  157.8 2.1 fusion.144
  164.7 2.4 fusion.151
  167.3 2.1 fusion.144
  174.2 2.4 fusion.151
  176.9 2.1 fusion.144
  183.8 2.4 fusion.151
  186.4 2.1 fusion.144
  193.3 2.4 fusion.151
  195.9 2.1 fusion.144
  202.8 2.4 fusion.151
  205.4 2.1 fusion.144
  212.3 2.4 fusion.151
  221.8 2.4 fusion.151
  224.5 2.1 fusion.144
  231.4 2.4 fusion.151
  234.0 2.1 fusion.144
  240.9 2.4 fusion.151
  243.5 2.1 fusion.144
  250.4 2.4 fusion.151
  259.9 2.4 fusion.151
  269.4 2.4 fusion.151
  272.0 2.1 fusion.144
  278.9 2.4 fusion.151
  281.5 2.1 fusion.144
  288.4 2.4 fusion.151
  291.0 2.1 fusion.144
  297.9 2.4 fusion.151
  300.5 2.1 fusion.144
  307.4 2.4 fusion.151
  317.0 2.4 fusion.151
  319.6 2.1 fusion.144
  326.5 2.4 fusion.151
  329.1 2.1 fusion.144
  336.0 2.4 fusion.151
  338.6 2.1 fusion.144
  345.5 2.4 fusion.151
  348.1 2.1 fusion.144
  355.0 2.4 fusion.151
  357.6 2.1 fusion.144
  364.5 2.4 fusion.151
  367.1 2.1 fusion.144
  374.0 2.4 fusion.151
  376.6 6.8 transpose.94
  383.5 270.7 %all-reduce.29.cloned.1.call-done = f32[884736]{0:T(1024)} async-done(((f32[884736]{0:T(1024)}), f32[884736]{0:T(1024)}) %all-reduce.29.cloned.1.call-update) | async-done | bytes 3538960 | tf_op jit(solution)/shard_map/psum | solution.py:70
  654.2 3.7 multiply_convert_fusion
  657.9 7.5 all_to_all.15
  666.1 12.0 reduce.50
  678.0 5.5 reshape.752
  683.5 13.2 %all-to-all-start = ((bf16[256,2,1728]{2,1,0:T(2,128)(2,1)}), bf16[256,2,1728]{2,1,0:T(2,128)(2,1)}, u32[]{:S(2)}, u32[]{:S(2)}) async-start(bf16[256,2,1728]{2,1,0:T(2,128)(2,1)} %reshape.752), calls=%async_computation | async-start | bytes 3670016 | tf_op jit(solution)/shard_map/all_to_all | solution.py:73
  697.5 85.0 %all-reduce.25 = f32[256]{0:T(256)S(1)} all-reduce(f32[256]{0:T(256)S(1)} %dynamic-update-slice.11), channel_id=1, replica_groups=mesh['samples'=256] {'samples'}, use_global_device_ids=true, to_apply=%add.25 | all-reduce | flops 256 | bytes 2048
  783.7 11.1 reshape.753
  796.7 250.1 %all-reduce.31.cloned.1.call-done = f32[256,256]{0,1:T(8,128)} async-done(((f32[256,256]{0,1:T(8,128)}), f32[256,256]{0,1:T(8,128)}) %all-reduce.31.cloned.1.call-update) | async-done | bytes 262160 | tf_op jit(solution)/shard_map/psum | solution.py:77
  1046.8 2.7 gather_fusion
  1051.9 11.7 cholesky.49
  1063.7 9.8 custom-call.18
  1074.0 11.7 cholesky.103
  1088.6 4.1 while.45
  1092.7 19.7 %custom-call.19 = f32[2,128,128]{1,2,0:T(8,128)S(1)} custom-call(f32[2,128,128]{2,1,0:T(8,128)S(1)} %get-tuple-element.324), custom_call_target="InvertDiagBlocksLowerTriangular" | custom-call | tf_op jit(solution)/shard_map/jit(_cho_solve)/triangular_solve | solution.py:57
  1113.5 2.9 fusion.49
  1117.0 77.6 %psum.23 = f32[]{:T(128)} all-reduce(f32[]{:T(128)} %multiply_reduce_fusion.3), channel_id=1, replica_groups=mesh['samples'=256] {'samples'}, use_global_device_ids=true, to_apply=%region_21.22 | all-reduce | flops 1 | bytes 8 | tf_op jit(solution)/shard_map/psum | solution.py:81
  (2399 shorter events, 266.4 us)
Async XLA Ops:
  6.5 3.0 copy-start
  6.5 647.6 %all-reduce.29.cloned.1.call-start = ((), (), s32[]{:S(2)}) async-start(), calls=%async_computation.1 | async-start | bytes 7077888 | tf_op jit(solution)/shard_map/psum | solution.py:70
  9.8 134.5 %copy-start.5 = (f32[64]{0:T(128)S(1)}, f32[64]{0:T(128)}, u32[]{:S(2)}) copy-start(f32[64]{0:T(128)} %param.13) | copy-start | bytes 772
  383.5 270.7 %copy-start.2 = (f32[884736]{0:T(1024)S(1)}, f32[884736]{0:T(1024)}, u32[]{:S(2)}) copy-start(f32[884736]{0:T(1024)} %transpose.94) | copy-start | bytes 10616836
  683.5 100.2 %all-to-all-start = ((bf16[256,2,1728]{2,1,0:T(2,128)(2,1)}), bf16[256,2,1728]{2,1,0:T(2,128)(2,1)}, u32[]{:S(2)}, u32[]{:S(2)}) async-start(bf16[256,2,1728]{2,1,0:T(2,128)(2,1)} %reshape.752), calls=%async_computation | async-start | bytes 3670016 | tf_op jit(solution)/shard_map/all_to_all | solution.py:73
  696.7 350.1 %all-reduce.31.cloned.1.call-start = ((), (), s32[]{:S(2)}) async-start(), calls=%async_computation.2 | async-start | bytes 524288 | tf_op jit(solution)/shard_map/psum | solution.py:77
  794.9 1.8 copy-start.4
  1046.8 5.1 copy-start.3
  1088.6 107.3 %copy-start.1 = (f32[9,64]{1,0:T(8,128)S(1)}, f32[9,64]{1,0:T(8,128)}, u32[]{:S(2)}) copy-start(f32[9,64]{1,0:T(8,128)} %param.11) | copy-start | bytes 6916
Sparse Core Ops, SparseCore 0:
  383.6 270.5 all-reduce.28
  796.8 249.9 all-reduce.30
where the time goes:
time: 1210 us; the launch traced here: 1200 us
  waiting for transfers between devices  521 us (43%)
  local copies, waits for them, and re-layouts  196 us (16%)
  blocking collectives  163 us (13%)
  matrix products  154 us (13%)
  other arithmetic  123 us (10%)
  between operations  17.4 us (1%)
  loops' own time  15.4 us (1%)
  starting transfers between devices  13.2 us (1%)
    psum x1, waiting for transfers between devices, per_device(): grad_total = lax.psum(jnp.sum(logderiv, axis=0), 'samples')  271 us
    psum x1, waiting for transfers between devices, per_device(): gram_matrix = lax.psum(partial_gram, 'samples')  250 us
    dot_general x72, matrix products, block_step(): jnp.einsum('kis,kio->os', shifted_copies(active, lattice_side), kernel, p...  148 us
    unnamed x1, blocking collectives  85 us
    dynamic_slice x240, local copies, waits for them, and re-layouts, log_amplitude(): lax.scan(lambda carry, kernel: (block_step(carry, kernel, lattice_side),...  83.2 us
    psum x1, blocking collectives, per_device(): square_total = lax.psum(jnp.sum(own_part * own_part), 'samples')  77.6 us
    another operation x7, other arithmetic, solve_coeffs(): factor = jnp.linalg.cholesky(system)  34.5 us
    another operation x465, local copies, waits for them, and re-layouts, shifted_copies(): jnp.stack(copies, 0).reshape(9, channels, lattice_side * lattice_side)  32.6 us
  transfers between devices with their start and end apart: 3, of which 2 were waited for; matrix products, arithmetic and copies ran while one was open for 0% of the time, Pallas kernels for 0%

commit v1 on v0

v1 whole, which is shorter than its diff:
```python
import math

import jax
import jax.numpy as jnp
from jax import lax
from jax.experimental import pallas as pl
from jax.experimental.pallas import tpu as pltpu
from jax.sharding import PartitionSpec as P

SIDE = 16
SITES = 256
CH = 64
LAYERS = 24
NS = 256
TAPS = 9
OWN_ROWS = 27
SEND_SUB = 4
SEND_TILES = 7
SEND_LANES = 128 * SEND_TILES
TOP = 32767.0
LAYER_ROWS = 288
P_SIZE = 884736

SHIFT_RATIO = 0.05
GELU_A = math.sqrt(2.0 / math.pi)
GELU_B = 0.044715

F32 = jnp.float32
BF16 = jnp.bfloat16


def split_two(values):
    high = values.astype(BF16)
    low = (values - high.astype(F32)).astype(BF16)
    return high, low


def matmul(a, b):
    return lax.dot_general(a, b, (((1,), (0,)), ((), ())), preferred_element_type=F32)


def matmul_nt(a, b):
    return lax.dot_general(a, b, (((1,), (1,)), ((), ())), preferred_element_type=F32)


def roll_lanes(values, amount):
    return pltpu.roll(values, amount % SITES, 1)


def shifted_copies(values, column):
    first, last = column == 0, column == SIDE - 1
    right = roll_lanes(values, 1)
    right_up, right_down = roll_lanes(right, -16), roll_lanes(right, 16)
    left = roll_lanes(values, -1)
    left_up, left_down = roll_lanes(left, -16), roll_lanes(left, 16)
    return [
        jnp.where(first, right, right_down),
        roll_lanes(values, 16),
        jnp.where(last, roll_lanes(left, 32), left_down),
        jnp.where(first, right_up, right),
        values,
        jnp.where(last, left_down, left),
        jnp.where(first, roll_lanes(right, -32), right_up),
        roll_lanes(values, -16),
        jnp.where(last, left, left_up),
    ]


def gather_back(parts, column):
    first, last = column == 0, column == SIDE - 1
    rows = [
        roll_lanes(parts[j], -16) + parts[3 + j] + roll_lanes(parts[6 + j], 16) for j in range(3)
    ]
    left = roll_lanes(rows[0], -1)
    right = roll_lanes(rows[2], 1)
    return (
        rows[1]
        + jnp.where(last, roll_lanes(left, 16), left)
        + jnp.where(first, roll_lanes(right, -16), right)
    )


def normalise(hidden):
    deviation = hidden - jnp.mean(hidden, axis=0, keepdims=True)
    scale = lax.rsqrt(jnp.mean(deviation * deviation, axis=0, keepdims=True) + 1e-05)
    return deviation * scale, scale


def activate(n):
    square = n * n
    t = jnp.tanh(GELU_A * (n + GELU_B * (n * square)))
    half = 0.5 * (1.0 + t)
    slope = half + (0.5 * GELU_A) * n * (1.0 - t * t) * (1.0 + (3.0 * GELU_B) * square)
    return n * half, slope


def normalise_back(grad, n, scale):
    return scale * (
        grad
        - jnp.mean(grad, axis=0, keepdims=True)
        - n * jnp.mean(grad * n, axis=0, keepdims=True)
    )


def encode_scale(largest):
    largest = jnp.maximum(largest, 1e-30)
    exponent = jnp.ceil(jnp.log(largest) * (1.0 / math.log(2.0)) + 0.006)
    mantissa = jnp.ceil(largest * jnp.exp2(-exponent) * 512.0 - 256.0)
    return exponent * 256.0 + jnp.clip(mantissa, 0.0, 255.0)


def decode_scale(code):
    exponent = jnp.floor(code * (1.0 / 256.0))
    return jnp.exp2(exponent) * ((code - 256.0 * exponent + 256.0) * (1.0 / 512.0))


def logderiv_kernel(
    spin_ref, embed_ref, readout_ref, kernels_hbm, out_ref,
    weights, u_hi, u_lo, n_all, slope_all, scale_all, rows, pair, sems,
):
    def fetch(layer):
        return pltpu.make_async_copy(kernels_hbm.at[layer], weights.at[layer], sems.at[layer])

    lax.fori_loop(0, LAYERS, lambda i, c: (fetch(i).start(), c)[1], 0)

    column = lax.broadcasted_iota(jnp.int32, (CH, SITES), 1) & (SIDE - 1)
    diagonal = lax.broadcasted_iota(jnp.int32, (CH, CH), 0) == lax.broadcasted_iota(
        jnp.int32, (CH, CH), 1
    )

    def as_column(row):
        return jnp.sum(jnp.where(diagonal, row, 0.0), axis=1, keepdims=True)

    spin = jnp.broadcast_to(spin_ref[...].astype(F32), (8, SITES))
    hidden = jnp.zeros((CH, SITES), F32)
    for k, copy in enumerate(shifted_copies(spin, column[:8])):
        hidden = hidden + as_column(embed_ref[k : k + 1, :]) * copy[0:1, :]

    def forward(layer, hidden):
        fetch(layer).wait()
        n, scale = normalise(hidden)
        u, slope = activate(n)
        n_all[layer] = n
        slope_all[layer] = slope
        scale_all[layer, 0:1, :] = scale
        for half in range(2):
            pair[half] = u[:, 128 * half : 128 * half + 128]
        mixed = jnp.concatenate(
            [
                jnp.concatenate([pair[half, pl.ds(odd, 32, stride=2), :] for half in range(2)], 1)
                for odd in range(2)
            ],
            0,
        )
        for k, copy in enumerate(shifted_copies(mixed, column)):
            high, low = split_two(copy)
            for odd in range(2):
                place = pl.ds(LAYER_ROWS * odd + 32 * k, 32)
                u_hi[layer, place, :] = high[32 * odd : 32 * odd + 32]
                u_lo[layer, place, :] = low[32 * odd : 32 * odd + 32]
        taps = jnp.concatenate(
            [weights[layer, pl.ds(odd, LAYER_ROWS, stride=2), :] for odd in range(2)], 0
        )
        w_hi, w_lo = split_two(taps.T)
        both = matmul(jnp.concatenate([w_hi, w_lo], 0), u_hi[layer])
        rest = matmul(w_hi, u_lo[layer])
        return hidden + (both[:CH] + (both[CH:] + rest))

    hidden = lax.fori_loop(0, LAYERS, forward, hidden)

    n, scale = normalise(hidden)
    _, slope = activate(n)
    grad = normalise_back((as_column(readout_ref[...]) * (1.0 / SIDE)) * slope, n, scale)
    zeros = jnp.zeros((CH, SITES), BF16)

    def backward(step, grad):
        layer = LAYERS - 1 - step
        high, low = split_two(grad)
        wide = jnp.concatenate(split_two(weights[layer]), 1)
        taps = matmul(
            jnp.concatenate([wide, wide], 1), jnp.concatenate([high, high, low, low], 0)
        )
        even = jnp.concatenate([high, zeros, low, zeros], 0)
        odd = jnp.concatenate([zeros, high, zeros, low], 0)
        top, bottom = pl.ds(0, LAYER_ROWS), pl.ds(LAYER_ROWS, LAYER_ROWS)
        main = matmul_nt(u_hi[layer, top, :], even) + matmul_nt(u_hi[layer, bottom, :], odd)
        rest = matmul_nt(u_lo[layer, top, :], even[:128]) + matmul_nt(u_lo[layer, bottom, :], odd[:128])
        entries = main[:, :128] + (main[:, 128:] + rest)
        rows[pl.ds(pl.multiple_of(layer * LAYER_ROWS, 8), LAYER_ROWS), :] = entries
        back = gather_back([taps[CH * k : CH * k + CH] for k in range(TAPS)], column)
        return grad + normalise_back(back * slope_all[layer], n_all[layer], scale_all[layer, 0:1, :])

    lax.fori_loop(0, LAYERS, backward, grad)

    spare = lax.broadcasted_iota(jnp.int32, (SEND_SUB, 128), 0) == SEND_SUB - 1

    def place_rows(block, carry):
        source = pl.multiple_of(block * (8 * OWN_ROWS), 8)
        for j in range(8):
            tiles = [
                rows[pl.ds(source + (OWN_ROWS * j + SEND_SUB * t), SEND_SUB), :]
                for t in range(SEND_TILES)
            ]
            tiles[-1] = jnp.where(spare, 0.0, tiles[-1])
            largest = jnp.abs(tiles[0])
            for tile in tiles[1:]:
                largest = jnp.maximum(largest, jnp.abs(tile))
            code = encode_scale(jnp.max(largest, axis=0, keepdims=True))
            factor = TOP / decode_scale(code)
            coded = [jnp.round(tile * factor) for tile in tiles]
            coded[-1] = jnp.where(spare, code, coded[-1])
            out_ref[block * 8 + j] = jnp.concatenate(coded, 1).astype(jnp.int32).astype(jnp.int16)
        return carry

    lax.fori_loop(0, NS // 8, place_rows, 0)


def logderiv_rows(spin, embedding, kernels, readout):
    vmem = pl.BlockSpec(memory_space=pltpu.VMEM)
    hbm = pl.BlockSpec(memory_space=pl.ANY)
    return pl.pallas_call(
        logderiv_kernel,
        out_shape=jax.ShapeDtypeStruct((NS, SEND_SUB, SEND_LANES), jnp.int16),
        in_specs=[vmem, vmem, vmem, hbm],
        out_specs=vmem,
        scratch_shapes=[
            pltpu.VMEM((LAYERS, TAPS * CH, CH), F32),
            pltpu.VMEM((LAYERS, TAPS * CH, SITES), BF16),
            pltpu.VMEM((LAYERS, TAPS * CH, SITES), BF16),
            pltpu.VMEM((LAYERS, CH, SITES), F32),
            pltpu.VMEM((LAYERS, CH, SITES), F32),
            pltpu.VMEM((LAYERS, 8, SITES), F32),
            pltpu.VMEM((LAYERS * LAYER_ROWS + 8, 128), F32),
            pltpu.VMEM((2, CH, 128), F32),
            pltpu.SemaphoreType.DMA((LAYERS,)),
        ],
        compiler_params=pltpu.CompilerParams(vmem_limit_bytes=60 << 20),
        name="logderiv",
    )(spin, embedding, readout, kernels.reshape(LAYERS, TAPS * CH, CH))


def gram_kernel(x_ref, centered_ref, gram_ref, values):
    lower = lax.broadcasted_iota(jnp.int32, (2 * SEND_SUB, 128), 0) < SEND_SUB

    def widen(block, carry):
        for j in range(4):
            first = block * 8 + 2 * j
            both = jnp.concatenate([x_ref[first + i].astype(jnp.int32).astype(F32) for i in range(2)], 0)
            code = both[:, SEND_LANES - 128 :]
            code = jnp.where(lower, code[SEND_SUB - 1 : SEND_SUB], code[2 * SEND_SUB - 1 : 2 * SEND_SUB])
            scale = decode_scale(code) * (1.0 / TOP)
            place = pl.ds(pl.multiple_of(first * SEND_SUB, 8), 2 * SEND_SUB)
            for t in range(SEND_TILES):
                values[t, place, :] = both[:, 128 * t : 128 * t + 128] * scale
        return carry

    lax.fori_loop(0, NS // 8, widen, 0)
    total = jnp.zeros((NS, NS), F32)
    held = None
    for r in range(OWN_ROWS):
        entries = values[r // SEND_SUB, pl.ds(r % SEND_SUB, NS, stride=SEND_SUB), :]
        mean = jnp.sum(entries, axis=0, keepdims=True) * (1.0 / NS)
        centered = ((entries - mean) * (1.0 / math.sqrt(NS))).astype(BF16)
        centered_ref[:, 128 * r : 128 * r + 128] = centered
        if held is None and r + 1 < OWN_ROWS:
            held = centered
        elif held is None:
            total = total + matmul_nt(centered, centered)
        else:
            wide = jnp.concatenate([held, centered], 1)
            total = total + matmul_nt(wide, wide)
            held = None
    gram_ref[...] = total


def partial_gram(x):
    vmem = pl.BlockSpec(memory_space=pltpu.VMEM)
    return pl.pallas_call(
        gram_kernel,
        out_shape=(
            jax.ShapeDtypeStruct((NS, OWN_ROWS * 128), BF16),
            jax.ShapeDtypeStruct((NS, NS), F32),
        ),
        in_specs=[vmem],
        out_specs=(vmem, vmem),
        scratch_shapes=[pltpu.VMEM((SEND_TILES, NS * SEND_SUB, 128), F32)],
        compiler_params=pltpu.CompilerParams(vmem_limit_bytes=40 << 20),
        name="partial_gram",
    )(x)


def direction_kernel(table_ref, centered_ref, out_ref, system):
    diagonal = lax.broadcasted_iota(jnp.int32, (NS, NS), 0) == lax.broadcasted_iota(
        jnp.int32, (NS, NS), 1
    )

    def total(values):
        return jnp.sum(values, axis=1, keepdims=True)

    def as_row(values):
        return jnp.sum(jnp.where(diagonal, values, 0.0), axis=0, keepdims=True)

    gram = table_ref[:, :NS]
    energy = as_row(table_ref[:, NS : NS + 1])
    spread = (energy - total(energy) * (1.0 / NS)) * (1.0 / math.sqrt(NS))
    diag_term = SHIFT_RATIO * (total(as_row(gram)) * (1.0 / NS)) + 1e-06
    system[...] = gram + jnp.where(diagonal, diag_term, 0.0)
    tiny = 1e-37

    def iterate(state):
        count, x, r, p, rr = state
        for _ in range(4):
            q = as_row(total(system[...] * p))
            alpha = rr / jnp.maximum(total(p * q), tiny)
            x = x + alpha * p
            r = r - alpha * q
            latest = total(r * r)
            p = r + (latest / jnp.maximum(rr, tiny)) * p
            rr = latest
        return count + 1, x, r, p, rr

    start = total(spread * spread)
    goal = start * 1e-13
    _, coeffs, _, _, _ = lax.while_loop(
        lambda state: (state[0] < 512) & ((state[4] - goal)[0, 0] > 0.0),
        iterate,
        (jnp.int32(0), jnp.zeros((1, NS), F32), spread, spread, start),
    )
    square_total = total(coeffs * as_row(total(table_ref[:, :NS] * coeffs)))
    high = coeffs.astype(BF16).astype(F32)
    middle = (coeffs - high).astype(BF16).astype(F32)
    low = coeffs - high - middle
    line = lax.broadcasted_iota(jnp.int32, (16, NS), 0)
    parts = jnp.where(line == 0, high, jnp.where(line == 1, middle, jnp.where(line == 2, low, 0.0)))
    own = jnp.sum(matmul(parts.astype(BF16), centered_ref[...]), axis=0, keepdims=True)
    out_ref[...] = own * lax.rsqrt(square_total * (1.0 / P_SIZE) + 1e-06)


def direction(table, centered):
    vmem = pl.BlockSpec(memory_space=pltpu.VMEM)
    return pl.pallas_call(
        direction_kernel,
        out_shape=jax.ShapeDtypeStruct((1, OWN_ROWS * 128), F32),
        in_specs=[vmem, vmem],
        out_specs=vmem,
        scratch_shapes=[pltpu.VMEM((NS, NS), F32)],
        compiler_params=pltpu.CompilerParams(vmem_limit_bytes=40 << 20),
        name="direction",
    )(table, centered)


def exchange(blocks):
    return lax.all_to_all(blocks, "samples", split_axis=0, concat_axis=0, tiled=True)


def per_device(spin_configs, energy, embedding, kernels, readout):
    own = logderiv_rows(spin_configs, embedding, kernels, readout.reshape(1, CH))
    centered, part = partial_gram(exchange(own))
    gram_row = jnp.sum(exchange(part.reshape(NS, 1, NS)), axis=0)
    line = jnp.concatenate([gram_row, jnp.broadcast_to(energy[:, None], (1, 128))], 1)
    table = exchange(jnp.broadcast_to(line[None], (NS, 1, NS + 128))).reshape(NS, NS + 128)
    return direction(table, centered).reshape(-1)


def solution(mesh):
    return jax.shard_map(
        per_device,
        mesh=mesh,
        in_specs=(P("samples", None), P("samples"), P(), P(), P()),
        out_specs=P("samples"),
        check_vma=False,
    )
```

time: 1210 us -> 160 us (0.13)
  waiting for transfers between devices: 521 us -> 14.8 us
  local copies, waits for them, and re-layouts: 196 us -> 1.22 us
  matrix products: 154 us -> 0 us
  other arithmetic: 123 us -> 0.93 us
  blocking collectives: 163 us -> 86.6 us
  Pallas kernels: 0 us -> 47.7 us
  between operations: 17.4 us -> 0.69 us
  loops' own time: 15.4 us -> 0 us
    psum x2 -> x0, waiting for transfers between devices: 521 us -> none  [the longest x1 271 us: per_device(): grad_total = lax.psum(jnp.sum(logderiv, axis=0), 'samples')]
    dot_general x75 -> x0, matrix products: 153 us -> none  [the longest x72 148 us: block_step(): jnp.einsum('kis,kio->os', shifted_copies(active, lattice_side), kernel, p...]
    all_to_all x0 -> x2, blocking collectives: none -> 86.6 us  [exchange(): lax.all_to_all(blocks, 'samples', split_axis=0, concat_axis=0, tiled=True)]
    unnamed x1 -> x0, blocking collectives: 85 us -> none
    dynamic_slice x240 -> x0, local copies, waits for them, and re-layouts: 83.2 us -> none  [log_amplitude(): lax.scan(lambda carry, kernel: (block_step(carry, kernel, lattice_side),...]
    psum x1 -> x0, blocking collectives: 77.6 us -> none  [per_device(): square_total = lax.psum(jnp.sum(own_part * own_part), 'samples')]
    another operation x17 -> x0, other arithmetic: 54.3 us -> none  [the longest x7 34.5 us: solve_coeffs(): factor = jnp.linalg.cholesky(system)]
    pallas_call x0 -> x3, Pallas kernels: none -> 47.7 us  [the longest x1 33.3 us: logderiv_rows(): pl.pallas_call(logderiv_kernel, out_shape=jax.ShapeDtypeStruct((NS, SEND_...]
  transfers between devices with their start and end apart: 3 -> 1, of which waited for: 2 -> 1; matrix products, arithmetic and copies ran while one was open for 0% -> 0% of each run, Pallas kernels for 0% -> 0%
where the time goes in v1:
time: 160 us; the launch traced here: 158 us
  blocking collectives  86.6 us (54%)
  Pallas kernels  47.7 us (30%)
  waiting for transfers between devices  14.8 us (9%)
  starting transfers between devices  6.29 us (4%)
    all_to_all x2, blocking collectives, exchange(): lax.all_to_all(blocks, 'samples', split_axis=0, concat_axis=0, tiled=True)  86.6 us
    pallas_call x1, Pallas kernels, logderiv_rows(): pl.pallas_call(logderiv_kernel, out_shape=jax.ShapeDtypeStruct((NS, SEND_...  33.3 us
    all_to_all x1, waiting for transfers between devices, exchange(): lax.all_to_all(blocks, 'samples', split_axis=0, concat_axis=0, tiled=True)  14.8 us
    pallas_call x1, Pallas kernels, direction(): pl.pallas_call(direction_kernel, out_shape=jax.ShapeDtypeStruct((1, OWN_R...  12.4 us
    all_to_all x1, starting transfers between devices, exchange(): lax.all_to_all(blocks, 'samples', split_axis=0, concat_axis=0, tiled=True)  6.29 us
  transfers between devices with their start and end apart: 1, of which 1 were waited for; matrix products, arithmetic and copies ran while one was open for 0% of the time, Pallas kernels for 0%

profile of v1, /device:TPU:1, one launch (start us, length us, event | category | flops | bytes accessed | tf_op | source)
XLA Modules:
  0.0 158.3 jit_solution(4840189613594845077)
XLA Ops:
  0.0 33.3 %logderiv.1 = s16[256,4,896]{2,1,0:T(4,128)(2,1)} custom-call(s32[1,256]{1,0:T(1,128)} %spin_ref.1, f32[9,64]{1,0:T(8,128)} %embed_ref.1, f32[1,64]{1,0:T(1,128)} %bitcast.13, f32[24,576,64]{2,1,0:T(8,128)} %bitcast.11), custom_call_target="tpu_custom_call" | custom-call | tf_op jit(solution)/shard_map/logderiv/pallas_call | solution.py:221
  33.3 63.5 %all_to_all.15.x_ref = s16[256,4,896]{2,1,0:T(4,128)(2,1)S(1)} all-to-all(s16[256,4,896]{2,1,0:T(4,128)(2,1)} %logderiv.1), channel_id=1, replica_groups=mesh['samples'=256] {'samples'}, dimensions={0} | all-to-all | bytes 3670016 | tf_op jit(solution)/shard_map/all_to_all | solution.py:353
  96.8 2.1 %partial_gram.1 = (bf16[256,3456]{1,0:T(8,128)(2,1)S(1)}, f32[256,256]{1,0:T(8,128)S(1)}) custom-call(s16[256,4,896]{2,1,0:T(4,128)(2,1)S(1)} %all_to_all.15.x_ref), custom_call_target="tpu_custom_call" | custom-call | tf_op jit(solution)/shard_map/partial_gram/pallas_call | solution.py:278
  98.9 1.0 copy.6
  99.9 6.3 %all-to-all-start.1 = ((f32[256,1,256]{2,1,0:T(1,128)}), f32[256,1,256]{2,1,0:T(1,128)S(1)}, u32[]{:S(2)}, u32[]{:S(2)}) async-start(f32[256,1,256]{2,1,0:T(1,128)} %copy.6), calls=%async_computation.1 | async-start | bytes 524288 | tf_op jit(solution)/shard_map/all_to_all | solution.py:353
  106.8 14.8 %all-to-all-done.1 = f32[256,1,256]{2,1,0:T(1,128)S(1)} async-done(((f32[256,1,256]{2,1,0:T(1,128)}), f32[256,1,256]{2,1,0:T(1,128)S(1)}, u32[]{:S(2)}, u32[]{:S(2)}) %all-to-all-start.1) | async-done | bytes 262176 | tf_op jit(solution)/shard_map/all_to_all | solution.py:353
  121.6 0.3 reduce_sum.11
  121.9 0.2 broadcast_in_dim.16
  122.1 23.1 %all_to_all.16 = f32[256,1,384]{2,1,0:T(1,128)S(1)} all-to-all(f32[256,1,384]{2,1,0:T(1,128)S(1)} %broadcast_in_dim.16), channel_id=1, replica_groups=mesh['samples'=256] {'samples'}, dimensions={0} | all-to-all | bytes 786432 | tf_op jit(solution)/shard_map/all_to_all | solution.py:353
  145.2 12.4 %direction.1 = f32[1,3456]{1,0:T(1,128)S(1)} custom-call(f32[256,384]{1,0:T(8,128)S(1)} %bitcast.9, bf16[256,3456]{1,0:T(8,128)(2,1)S(1)} %get-tuple-element.8.centered_ref), custom_call_target="tpu_custom_call" | custom-call | tf_op jit(solution)/shard_map/direction/pallas_call | solution.py:341
  157.6 0.6 reduce.2
  (2 shorter events, 0.0 us)
Async XLA Ops:
  99.9 21.7 %all-to-all-start.1 = ((f32[256,1,256]{2,1,0:T(1,128)}), f32[256,1,256]{2,1,0:T(1,128)S(1)}, u32[]{:S(2)}, u32[]{:S(2)}) async-start(f32[256,1,256]{2,1,0:T(1,128)} %copy.6), calls=%async_computation.1 | async-start | bytes 524288 | tf_op jit(solution)/shard_map/all_to_all | solution.py:353

commit v2 on v1

--- a/solution.py
+++ b/solution.py
@@ -15,6 +15,7 @@
 TAPS = 9
 OWN_ROWS = 27
 SEND_SUB = 4
+STEP_CHUNKS = 11
 SEND_TILES = 7
 SEND_LANES = 128 * SEND_TILES
 TOP = 32767.0
@@ -128,6 +129,8 @@
         jnp.int32, (CH, CH), 1
     )
 
+    unit = jnp.where(diagonal, 1.0, 0.0).astype(BF16)
+
     def as_column(row):
         return jnp.sum(jnp.where(diagonal, row, 0.0), axis=1, keepdims=True)
 
@@ -152,16 +155,15 @@
             ],
             0,
         )
-        for k, copy in enumerate(shifted_copies(mixed, column)):
-            high, low = split_two(copy)
-            for odd in range(2):
-                place = pl.ds(LAYER_ROWS * odd + 32 * k, 32)
-                u_hi[layer, place, :] = high[32 * odd : 32 * odd + 32]
-                u_lo[layer, place, :] = low[32 * odd : 32 * odd + 32]
+        for store, part in zip((u_hi, u_lo), split_two(mixed)):
+            for k, copy in enumerate(shifted_copies(part, column)):
+                for odd in range(2):
+                    place = pl.ds(LAYER_ROWS * odd + 32 * k, 32)
+                    store[layer, place, :] = copy[32 * odd : 32 * odd + 32]
         taps = jnp.concatenate(
             [weights[layer, pl.ds(odd, LAYER_ROWS, stride=2), :] for odd in range(2)], 0
         )
-        w_hi, w_lo = split_two(taps.T)
+        w_hi, w_lo = [matmul_nt(unit, part).astype(BF16) for part in split_two(taps)]
         both = matmul(jnp.concatenate([w_hi, w_lo], 0), u_hi[layer])
         rest = matmul(w_hi, u_lo[layer])
         return hidden + (both[:CH] + (both[CH:] + rest))
@@ -173,8 +175,25 @@
     grad = normalise_back((as_column(readout_ref[...]) * (1.0 / SIDE)) * slope, n, scale)
     zeros = jnp.zeros((CH, SITES), BF16)
 
+    spare = lax.broadcasted_iota(jnp.int32, (SEND_SUB, 128), 0) == SEND_SUB - 1
+
+    def place_chunk(chunk):
+        tiles = [rows[pl.ds(chunk * OWN_ROWS + SEND_SUB * t, SEND_SUB), :] for t in range(SEND_TILES)]
+        tiles[-1] = jnp.where(spare, 0.0, tiles[-1])
+        largest = jnp.abs(tiles[0])
+        for tile in tiles[1:]:
+            largest = jnp.maximum(largest, jnp.abs(tile))
+        code = encode_scale(jnp.max(largest, axis=0, keepdims=True))
+        factor = TOP / decode_scale(code)
+        coded = [jnp.round(tile * factor) for tile in tiles]
+        coded[-1] = jnp.where(spare, code, coded[-1])
+        out_ref[chunk] = jnp.concatenate(coded, 1).astype(jnp.int32).astype(jnp.int16)
+
     def backward(step, grad):
         layer = LAYERS - 1 - step
+        first = (LAYER_ROWS * (layer + 1) + OWN_ROWS - 1) // OWN_ROWS
+        for j in range(STEP_CHUNKS):
+            place_chunk(jnp.minimum(first + j, NS - 1))
         high, low = split_two(grad)
         wide = jnp.concatenate(split_two(weights[layer]), 1)
         taps = matmul(
@@ -192,27 +211,8 @@
 
     lax.fori_loop(0, LAYERS, backward, grad)
 
-    spare = lax.broadcasted_iota(jnp.int32, (SEND_SUB, 128), 0) == SEND_SUB - 1
-
-    def place_rows(block, carry):
-        source = pl.multiple_of(block * (8 * OWN_ROWS), 8)
-        for j in range(8):
-            tiles = [
-                rows[pl.ds(source + (OWN_ROWS * j + SEND_SUB * t), SEND_SUB), :]
-                for t in range(SEND_TILES)
-            ]
-            tiles[-1] = jnp.where(spare, 0.0, tiles[-1])
-            largest = jnp.abs(tiles[0])
-            for tile in tiles[1:]:
-                largest = jnp.maximum(largest, jnp.abs(tile))
-            code = encode_scale(jnp.max(largest, axis=0, keepdims=True))
-            factor = TOP / decode_scale(code)
-            coded = [jnp.round(tile * factor) for tile in tiles]
-            coded[-1] = jnp.where(spare, code, coded[-1])
-            out_ref[block * 8 + j] = jnp.concatenate(coded, 1).astype(jnp.int32).astype(jnp.int16)
-        return carry
-
-    lax.fori_loop(0, NS // 8, place_rows, 0)
+    for chunk in range(STEP_CHUNKS):
+        place_chunk(chunk)
 
 
 def logderiv_rows(spin, embedding, kernels, readout):
@@ -270,7 +270,7 @@
             wide = jnp.concatenate([held, centered], 1)
             total = total + matmul_nt(wide, wide)
             held = None
-    gram_ref[...] = total
+    gram_ref[:, 0, :] = total
 
 
 def partial_gram(x):
@@ -279,7 +279,7 @@
         gram_kernel,
         out_shape=(
             jax.ShapeDtypeStruct((NS, OWN_ROWS * 128), BF16),
-            jax.ShapeDtypeStruct((NS, NS), F32),
+            jax.ShapeDtypeStruct((NS, 1, NS), F32),
         ),
         in_specs=[vmem],
         out_specs=(vmem, vmem),
@@ -289,13 +289,16 @@
     )(x)
 
 
-def direction_kernel(table_ref, centered_ref, out_ref, system):
+def direction_kernel(table_ref, centered_ref, out_ref, system, r_col, s_col):
     diagonal = lax.broadcasted_iota(jnp.int32, (NS, NS), 0) == lax.broadcasted_iota(
         jnp.int32, (NS, NS), 1
     )
 
     def total(values):
         return jnp.sum(values, axis=1, keepdims=True)
+
+    def as_column(values):
+        return total(jnp.where(diagonal, values, 0.0))
 
     def as_row(values):
         return jnp.sum(jnp.where(diagonal, values, 0.0), axis=0, keepdims=True)
@@ -307,24 +310,38 @@
     system[...] = gram + jnp.where(diagonal, diag_term, 0.0)
     tiny = 1e-37
 
+    def twice(values):
+        return jnp.concatenate([values, values], 1)
+
     def iterate(state):
-        count, x, r, p, rr = state
+        count, x, r, p, s, last, alpha, _ = state
         for _ in range(4):
-            q = as_row(total(system[...] * p))
-            alpha = rr / jnp.maximum(total(p * q), tiny)
-            x = x + alpha * p
-            r = r - alpha * q
-            latest = total(r * r)
-            p = r + (latest / jnp.maximum(rr, tiny)) * p
-            rr = latest
-        return count + 1, x, r, p, rr
-
-    start = total(spread * spread)
+            w_col = total(system[...] * r)
+            r_all = r_col[...]
+            norm = jnp.sum(r_all * r_all, axis=0, keepdims=True)
+            delta = jnp.sum(r_all * w_col, axis=0, keepdims=True)
+            beta = norm / jnp.maximum(last, tiny)
+            alpha = norm / jnp.maximum(delta - beta * norm / jnp.maximum(alpha, tiny), tiny)
+            last = norm
+            s_all = w_col + beta * s_col[...]
+            s_col[...] = s_all
+            r_col[...] = r_all - alpha * s_all
+            p = r + twice(beta) * p
+            s = as_row(w_col) + twice(beta) * s
+            x = x + twice(alpha) * p
+            r = r - twice(alpha) * s
+        return count + 1, x, r, p, s, last, alpha, norm
+
+    spread_col = jnp.broadcast_to(as_column(spread), (NS, 128))
+    r_col[...] = spread_col
+    s_col[...] = jnp.zeros((NS, 128), F32)
+    start = jnp.sum(spread_col * spread_col, axis=0, keepdims=True)
     goal = start * 1e-13
-    _, coeffs, _, _, _ = lax.while_loop(
-        lambda state: (state[0] < 512) & ((state[4] - goal)[0, 0] > 0.0),
+    zero = jnp.zeros((1, NS), F32)
+    _, coeffs, _, _, _, _, _, _ = lax.while_loop(
+        lambda state: (state[0] < 512) & ((state[7] - goal)[0, 0] > 0.0),
         iterate,
-        (jnp.int32(0), jnp.zeros((1, NS), F32), spread, spread, start),
+        (jnp.int32(0), zero, spread, zero, zero, jnp.full((1, 128), 1e30, F32), jnp.ones((1, 128), F32), start),
     )
     square_total = total(coeffs * as_row(total(table_ref[:, :NS] * coeffs)))
     high = coeffs.astype(BF16).astype(F32)
@@ -333,17 +350,17 @@
     line = lax.broadcasted_iota(jnp.int32, (16, NS), 0)
     parts = jnp.where(line == 0, high, jnp.where(line == 1, middle, jnp.where(line == 2, low, 0.0)))
     own = jnp.sum(matmul(parts.astype(BF16), centered_ref[...]), axis=0, keepdims=True)
-    out_ref[...] = own * lax.rsqrt(square_total * (1.0 / P_SIZE) + 1e-06)
+    out_ref[...] = (own * lax.rsqrt(square_total * (1.0 / P_SIZE) + 1e-06))[0]
 
 
 def direction(table, centered):
     vmem = pl.BlockSpec(memory_space=pltpu.VMEM)
     return pl.pallas_call(
         direction_kernel,
-        out_shape=jax.ShapeDtypeStruct((1, OWN_ROWS * 128), F32),
+        out_shape=jax.ShapeDtypeStruct((OWN_ROWS * 128,), F32),
         in_specs=[vmem, vmem],
         out_specs=vmem,
-        scratch_shapes=[pltpu.VMEM((NS, NS), F32)],
+        scratch_shapes=[pltpu.VMEM((NS, NS), F32), pltpu.VMEM((NS, 128), F32), pltpu.VMEM((NS, 128), F32)],
         compiler_params=pltpu.CompilerParams(vmem_limit_bytes=40 << 20),
         name="direction",
     )(table, centered)
@@ -356,10 +373,10 @@
 def per_device(spin_configs, energy, embedding, kernels, readout):
     own = logderiv_rows(spin_configs, embedding, kernels, readout.reshape(1, CH))
     centered, part = partial_gram(exchange(own))
-    gram_row = jnp.sum(exchange(part.reshape(NS, 1, NS)), axis=0)
+    gram_row = jnp.sum(exchange(part), axis=0)
     line = jnp.concatenate([gram_row, jnp.broadcast_to(energy[:, None], (1, 128))], 1)
     table = exchange(jnp.broadcast_to(line[None], (NS, 1, NS + 128))).reshape(NS, NS + 128)
-    return direction(table, centered).reshape(-1)
+    return direction(table, centered)
 
 
 def solution(mesh):

time: 160 us -> 151 us (0.944)
  Pallas kernels: 47.7 us -> 41.3 us
    pallas_call x1, Pallas kernels: 12.4 us -> 8.36 us  [direction(): pl.pallas_call(direction_kernel, out_shape=jax.ShapeDtypeStruct((OWN_ROWS...]
    pallas_call x1, Pallas kernels: 33.3 us -> 30.2 us  [logderiv_rows(): pl.pallas_call(logderiv_kernel, out_shape=jax.ShapeDtypeStruct((NS, SEND_...]
where the time goes in v2:
time: 151 us; the launch traced here: 150 us
  blocking collectives  86.6 us (57%)
  Pallas kernels  41.3 us (27%)
  waiting for transfers between devices  14.8 us (10%)
  starting transfers between devices  6.29 us (4%)
    all_to_all x2, blocking collectives, exchange(): lax.all_to_all(blocks, 'samples', split_axis=0, concat_axis=0, tiled=True)  86.6 us
    pallas_call x1, Pallas kernels, logderiv_rows(): pl.pallas_call(logderiv_kernel, out_shape=jax.ShapeDtypeStruct((NS, SEND_...  30.2 us
    all_to_all x1, waiting for transfers between devices, exchange(): lax.all_to_all(blocks, 'samples', split_axis=0, concat_axis=0, tiled=True)  14.8 us
    pallas_call x1, Pallas kernels, direction(): pl.pallas_call(direction_kernel, out_shape=jax.ShapeDtypeStruct((OWN_ROWS...  8.36 us
    all_to_all x1, starting transfers between devices, exchange(): lax.all_to_all(blocks, 'samples', split_axis=0, concat_axis=0, tiled=True)  6.29 us
  transfers between devices with their start and end apart: 1, of which 1 were waited for; matrix products, arithmetic and copies ran while one was open for 0% of the time, Pallas kernels for 0%

profile of v2, /device:TPU:1, one launch (start us, length us, event | category | flops | bytes accessed | tf_op | source)
XLA Modules:
  0.0 150.2 jit_solution(13417829394545875147)
XLA Ops:
  0.0 30.2 %logderiv.1 = s16[256,4,896]{2,1,0:T(4,128)(2,1)} custom-call(s32[1,256]{1,0:T(1,128)} %spin_ref.1, f32[9,64]{1,0:T(8,128)} %embed_ref.1, f32[1,64]{1,0:T(1,128)} %bitcast.11, f32[24,576,64]{2,1,0:T(8,128)} %bitcast.9), custom_call_target="tpu_custom_call" | custom-call | tf_op jit(solution)/shard_map/logderiv/pallas_call | solution.py:221
  30.2 63.5 %all_to_all.15.x_ref = s16[256,4,896]{2,1,0:T(4,128)(2,1)S(1)} all-to-all(s16[256,4,896]{2,1,0:T(4,128)(2,1)} %logderiv.1), channel_id=1, replica_groups=mesh['samples'=256] {'samples'}, dimensions={0} | all-to-all | bytes 3670016 | tf_op jit(solution)/shard_map/all_to_all | solution.py:370
  93.7 2.8 %partial_gram.1 = (bf16[256,3456]{1,0:T(8,128)(2,1)S(1)}, f32[256,1,256]{2,1,0:T(1,128)}) custom-call(s16[256,4,896]{2,1,0:T(4,128)(2,1)S(1)} %all_to_all.15.x_ref), custom_call_target="tpu_custom_call" | custom-call | tf_op jit(solution)/shard_map/partial_gram/pallas_call | solution.py:278
  96.5 6.3 %all-to-all-start.1 = ((f32[256,1,256]{2,1,0:T(1,128)}), f32[256,1,256]{2,1,0:T(1,128)S(1)}, u32[]{:S(2)}, u32[]{:S(2)}) async-start(f32[256,1,256]{2,1,0:T(1,128)} %get-tuple-element.7), calls=%async_computation.1 | async-start | bytes 524288 | tf_op jit(solution)/shard_map/all_to_all | solution.py:370
  103.4 14.8 %all-to-all-done.1 = f32[256,1,256]{2,1,0:T(1,128)S(1)} async-done(((f32[256,1,256]{2,1,0:T(1,128)}), f32[256,1,256]{2,1,0:T(1,128)S(1)}, u32[]{:S(2)}, u32[]{:S(2)}) %all-to-all-start.1) | async-done | bytes 262176 | tf_op jit(solution)/shard_map/all_to_all | solution.py:370
  118.2 0.3 reduce_sum.11
  118.5 0.2 broadcast_in_dim.16
  118.7 23.1 %all_to_all.16 = f32[256,1,384]{2,1,0:T(1,128)S(1)} all-to-all(f32[256,1,384]{2,1,0:T(1,128)S(1)} %broadcast_in_dim.16), channel_id=1, replica_groups=mesh['samples'=256] {'samples'}, dimensions={0} | all-to-all | bytes 786432 | tf_op jit(solution)/shard_map/all_to_all | solution.py:370
  141.8 8.4 %direction.1 = f32[3456]{0:T(1024)} custom-call(f32[256,384]{1,0:T(8,128)S(1)} %bitcast.8, bf16[256,3456]{1,0:T(8,128)(2,1)S(1)} %get-tuple-element.8.centered_ref), custom_call_target="tpu_custom_call" | custom-call | tf_op jit(solution)/shard_map/direction/pallas_call | solution.py:358
  (2 shorter events, 0.0 us)
Async XLA Ops:
  96.5 21.7 %all-to-all-start.1 = ((f32[256,1,256]{2,1,0:T(1,128)}), f32[256,1,256]{2,1,0:T(1,128)S(1)}, u32[]{:S(2)}, u32[]{:S(2)}) async-start(f32[256,1,256]{2,1,0:T(1,128)} %get-tuple-element.7), calls=%async_computation.1 | async-start | bytes 524288 | tf_op jit(solution)/shard_map/all_to_all | solution.py:370

commit v3 on v2

--- a/solution.py
+++ b/solution.py
@@ -9,10 +9,13 @@
 
 SIDE = 16
 SITES = 256
+HALF = 128
 CH = 64
 LAYERS = 24
 NS = 256
 TAPS = 9
+STEPS = (1, 0, -1)
+WIDE = 192
 OWN_ROWS = 27
 SEND_SUB = 4
 STEP_CHUNKS = 11
@@ -45,40 +48,39 @@
 
 
 def roll_lanes(values, amount):
-    return pltpu.roll(values, amount % SITES, 1)
-
-
-def shifted_copies(values, column):
-    first, last = column == 0, column == SIDE - 1
-    right = roll_lanes(values, 1)
-    right_up, right_down = roll_lanes(right, -16), roll_lanes(right, 16)
-    left = roll_lanes(values, -1)
-    left_up, left_down = roll_lanes(left, -16), roll_lanes(left, 16)
-    return [
-        jnp.where(first, right, right_down),
-        roll_lanes(values, 16),
-        jnp.where(last, roll_lanes(left, 32), left_down),
-        jnp.where(first, right_up, right),
-        values,
-        jnp.where(last, left_down, left),
-        jnp.where(first, roll_lanes(right, -32), right_up),
-        roll_lanes(values, -16),
-        jnp.where(last, left, left_up),
-    ]
-
-
-def gather_back(parts, column):
-    first, last = column == 0, column == SIDE - 1
-    rows = [
-        roll_lanes(parts[j], -16) + parts[3 + j] + roll_lanes(parts[6 + j], 16) for j in range(3)
-    ]
-    left = roll_lanes(rows[0], -1)
-    right = roll_lanes(rows[2], 1)
-    return (
-        rows[1]
-        + jnp.where(last, roll_lanes(left, 16), left)
-        + jnp.where(first, roll_lanes(right, -16), right)
-    )
+    return pltpu.roll(values, amount % HALF, 1)
+
+
+def halves(values):
+    return values[:, :HALF], values[:, HALF:]
+
+
+def join(even, odd):
+    return jnp.concatenate([even, odd], 1)
+
+
+def column_before(odd, place):
+    return jnp.where(place == 0, roll_lanes(odd, -7), roll_lanes(odd, 1))
+
+
+def column_after(even, place):
+    return jnp.where(place == 7, roll_lanes(even, 7), roll_lanes(even, -1))
+
+
+def column_roll(values, step, place):
+    even, odd = halves(values)
+    if step == 1:
+        return join(column_before(odd, place), even)
+    if step == -1:
+        return join(odd, column_after(even, place))
+    return values
+
+
+def row_roll(values, step):
+    if step == 0:
+        return values
+    even, odd = halves(values)
+    return join(roll_lanes(even, 8 * step), roll_lanes(odd, 8 * step))
 
 
 def normalise(hidden):
@@ -124,19 +126,22 @@
 
     lax.fori_loop(0, LAYERS, lambda i, c: (fetch(i).start(), c)[1], 0)
 
-    column = lax.broadcasted_iota(jnp.int32, (CH, SITES), 1) & (SIDE - 1)
+    place = lax.broadcasted_iota(jnp.int32, (CH, HALF), 1) & 7
     diagonal = lax.broadcasted_iota(jnp.int32, (CH, CH), 0) == lax.broadcasted_iota(
         jnp.int32, (CH, CH), 1
     )
 
-    unit = jnp.where(diagonal, 1.0, 0.0).astype(BF16)
-
     def as_column(row):
         return jnp.sum(jnp.where(diagonal, row, 0.0), axis=1, keepdims=True)
 
-    spin = jnp.broadcast_to(spin_ref[...].astype(F32), (8, SITES))
+    source = lax.broadcasted_iota(jnp.int32, (SITES, SITES), 0)
+    target = lax.broadcasted_iota(jnp.int32, (SITES, SITES), 1)
+    wanted = ((target & 127) >> 3) * SIDE + 2 * (target & 7) + (target >> 7)
+    order = jnp.where(source == wanted, 1.0, 0.0).astype(BF16)
+    spin = matmul(jnp.broadcast_to(spin_ref[...].astype(F32), (16, SITES)).astype(BF16), order)[:8]
     hidden = jnp.zeros((CH, SITES), F32)
-    for k, copy in enumerate(shifted_copies(spin, column[:8])):
+    for k in range(TAPS):
+        copy = row_roll(column_roll(spin, STEPS[k % 3], place[:8]), STEPS[k // 3])
         hidden = hidden + as_column(embed_ref[k : k + 1, :]) * copy[0:1, :]
 
     def forward(layer, hidden):
@@ -156,24 +161,35 @@
             0,
         )
         for store, part in zip((u_hi, u_lo), split_two(mixed)):
-            for k, copy in enumerate(shifted_copies(part, column)):
-                for odd in range(2):
-                    place = pl.ds(LAYER_ROWS * odd + 32 * k, 32)
-                    store[layer, place, :] = copy[32 * odd : 32 * odd + 32]
-        taps = jnp.concatenate(
-            [weights[layer, pl.ds(odd, LAYER_ROWS, stride=2), :] for odd in range(2)], 0
-        )
-        w_hi, w_lo = [matmul_nt(unit, part).astype(BF16) for part in split_two(taps)]
-        both = matmul(jnp.concatenate([w_hi, w_lo], 0), u_hi[layer])
-        rest = matmul(w_hi, u_lo[layer])
-        return hidden + (both[:CH] + (both[CH:] + rest))
+            for i, step in enumerate(STEPS):
+                store[layer, pl.ds(CH * i, CH), :] = row_roll(part, step)
+        groups = [
+            split_two(
+                jnp.concatenate(
+                    [
+                        weights[layer, pl.ds(CH * (3 * i + j) + odd, 32, stride=2), :]
+                        for i in range(3)
+                        for odd in range(2)
+                    ],
+                    0,
+                )
+            )
+            for j in range(3)
+        ]
+        w_hi, w_lo = [
+            jnp.concatenate([group[i].T for group in groups], 0)
+            for i in range(2)
+        ]
+        sums = matmul(w_hi, u_hi[layer]) + (matmul(w_hi, u_lo[layer]) + matmul(w_lo, u_hi[layer]))
+        moved = [column_roll(sums[CH * i : CH * i + CH], step, place) for i, step in enumerate(STEPS)]
+        return hidden + (moved[0] + moved[1] + moved[2])
 
     hidden = lax.fori_loop(0, LAYERS, forward, hidden)
 
     n, scale = normalise(hidden)
     _, slope = activate(n)
     grad = normalise_back((as_column(readout_ref[...]) * (1.0 / SIDE)) * slope, n, scale)
-    zeros = jnp.zeros((CH, SITES), BF16)
+    left = lax.broadcasted_iota(jnp.int32, (32, 128), 1) < CH
 
     spare = lax.broadcasted_iota(jnp.int32, (SEND_SUB, 128), 0) == SEND_SUB - 1
 
@@ -195,18 +211,36 @@
         for j in range(STEP_CHUNKS):
             place_chunk(jnp.minimum(first + j, NS - 1))
         high, low = split_two(grad)
-        wide = jnp.concatenate(split_two(weights[layer]), 1)
-        taps = matmul(
-            jnp.concatenate([wide, wide], 1), jnp.concatenate([high, high, low, low], 0)
-        )
-        even = jnp.concatenate([high, zeros, low, zeros], 0)
-        odd = jnp.concatenate([zeros, high, zeros, low], 0)
-        top, bottom = pl.ds(0, LAYER_ROWS), pl.ds(LAYER_ROWS, LAYER_ROWS)
-        main = matmul_nt(u_hi[layer, top, :], even) + matmul_nt(u_hi[layer, bottom, :], odd)
-        rest = matmul_nt(u_lo[layer, top, :], even[:128]) + matmul_nt(u_lo[layer, bottom, :], odd[:128])
-        entries = main[:, :128] + (main[:, 128:] + rest)
-        rows[pl.ds(pl.multiple_of(layer * LAYER_ROWS, 8), LAYER_ROWS), :] = entries
-        back = gather_back([taps[CH * k : CH * k + CH] for k in range(TAPS)], column)
+        g_hi, g_lo = [
+            jnp.concatenate([column_roll(part, -step, place) for step in STEPS], 0)
+            for part in (high, low)
+        ]
+        w_hi, w_lo = [
+            jnp.concatenate(
+                [
+                    jnp.concatenate([part[CH * (3 * i + j) : CH * (3 * i + j) + CH] for j in range(3)], 1)
+                    for i in range(3)
+                ],
+                0,
+            )
+            for part in split_two(weights[layer])
+        ]
+        sums = matmul(w_hi, g_hi) + (matmul(w_hi, g_lo) + matmul(w_lo, g_hi))
+        x_hi, x_lo = [jnp.concatenate([part, part[128:]], 0) for part in (g_hi, g_lo)]
+        both = matmul_nt(jnp.concatenate([u_hi[layer], u_lo[layer]], 0), x_hi)
+        products = both[:WIDE] + (both[WIDE:] + matmul_nt(u_hi[layer], x_lo))
+        for i in range(3):
+            even, odd = products[CH * i : CH * i + 32], products[CH * i + 32 : CH * i + CH]
+            packed = (
+                jnp.where(left, even[:, :128], pltpu.roll(odd[:, :128], CH, 1)),
+                jnp.where(left, pltpu.roll(even[:, :128], CH, 1), odd[:, :128]),
+                jnp.where(left, even[:, 128:], odd[:, 128:]),
+            )
+            for j in range(3):
+                target_rows = pl.multiple_of(layer * LAYER_ROWS + 32 * (3 * i + j), 8)
+                rows[pl.ds(target_rows, 32), :] = packed[j]
+        turned = [row_roll(sums[CH * i : CH * i + CH], -step) for i, step in enumerate(STEPS)]
+        back = turned[0] + turned[1] + turned[2]
         return grad + normalise_back(back * slope_all[layer], n_all[layer], scale_all[layer, 0:1, :])
 
     lax.fori_loop(0, LAYERS, backward, grad)
@@ -225,8 +259,8 @@
         out_specs=vmem,
         scratch_shapes=[
             pltpu.VMEM((LAYERS, TAPS * CH, CH), F32),
-            pltpu.VMEM((LAYERS, TAPS * CH, SITES), BF16),
-            pltpu.VMEM((LAYERS, TAPS * CH, SITES), BF16),
+            pltpu.VMEM((LAYERS, WIDE, SITES), BF16),
+            pltpu.VMEM((LAYERS, WIDE, SITES), BF16),
             pltpu.VMEM((LAYERS, CH, SITES), F32),
             pltpu.VMEM((LAYERS, CH, SITES), F32),
             pltpu.VMEM((LAYERS, 8, SITES), F32),

time: 151 us -> 147 us (0.974)
  Pallas kernels: 41.3 us -> 37.9 us
    pallas_call x1, Pallas kernels: 30.2 us -> 26.2 us  [logderiv_rows(): pl.pallas_call(logderiv_kernel, out_shape=jax.ShapeDtypeStruct((NS, SEND_...]
where the time goes in v3:
time: 147 us
  blocking collectives  86.6 us (59%)
  Pallas kernels  37.9 us (26%)
  waiting for transfers between devices  14.8 us (10%)
  starting transfers between devices  6.29 us (4%)
    all_to_all x2, blocking collectives, exchange(): lax.all_to_all(blocks, 'samples', split_axis=0, concat_axis=0, tiled=True)  86.6 us
    pallas_call x1, Pallas kernels, logderiv_rows(): pl.pallas_call(logderiv_kernel, out_shape=jax.ShapeDtypeStruct((NS, SEND_...  26.2 us
    all_to_all x1, waiting for transfers between devices, exchange(): lax.all_to_all(blocks, 'samples', split_axis=0, concat_axis=0, tiled=True)  14.8 us
    pallas_call x1, Pallas kernels, direction(): pl.pallas_call(direction_kernel, out_shape=jax.ShapeDtypeStruct((OWN_ROWS...  8.95 us
    all_to_all x1, starting transfers between devices, exchange(): lax.all_to_all(blocks, 'samples', split_axis=0, concat_axis=0, tiled=True)  6.29 us
  transfers between devices with their start and end apart: 1, of which 1 were waited for; matrix products, arithmetic and copies ran while one was open for 0% of the time, Pallas kernels for 0%

profile of v3, /device:TPU:1, one launch (start us, length us, event | category | flops | bytes accessed | tf_op | source)
XLA Modules:
  0.0 146.8 jit_solution(4077433559843693404)
XLA Ops:
  0.0 26.2 %logderiv.1 = s16[256,4,896]{2,1,0:T(4,128)(2,1)} custom-call(s32[1,256]{1,0:T(1,128)} %spin_ref.1, f32[9,64]{1,0:T(8,128)} %embed_ref.1, f32[1,64]{1,0:T(1,128)} %bitcast.11, f32[24,576,64]{2,1,0:T(8,128)} %bitcast.9), custom_call_target="tpu_custom_call" | custom-call | tf_op jit(solution)/shard_map/logderiv/pallas_call | solution.py:255
  26.2 63.5 %all_to_all.15.x_ref = s16[256,4,896]{2,1,0:T(4,128)(2,1)S(1)} all-to-all(s16[256,4,896]{2,1,0:T(4,128)(2,1)} %logderiv.1), channel_id=1, replica_groups=mesh['samples'=256] {'samples'}, dimensions={0} | all-to-all | bytes 3670016 | tf_op jit(solution)/shard_map/all_to_all | solution.py:404
  89.7 2.8 %partial_gram.1 = (bf16[256,3456]{1,0:T(8,128)(2,1)S(1)}, f32[256,1,256]{2,1,0:T(1,128)}) custom-call(s16[256,4,896]{2,1,0:T(4,128)(2,1)S(1)} %all_to_all.15.x_ref), custom_call_target="tpu_custom_call" | custom-call | tf_op jit(solution)/shard_map/partial_gram/pallas_call | solution.py:312
  92.5 6.3 %all-to-all-start.1 = ((f32[256,1,256]{2,1,0:T(1,128)}), f32[256,1,256]{2,1,0:T(1,128)S(1)}, u32[]{:S(2)}, u32[]{:S(2)}) async-start(f32[256,1,256]{2,1,0:T(1,128)} %get-tuple-element.7), calls=%async_computation.1 | async-start | bytes 524288 | tf_op jit(solution)/shard_map/all_to_all | solution.py:404
  99.4 14.8 %all-to-all-done.1 = f32[256,1,256]{2,1,0:T(1,128)S(1)} async-done(((f32[256,1,256]{2,1,0:T(1,128)}), f32[256,1,256]{2,1,0:T(1,128)S(1)}, u32[]{:S(2)}, u32[]{:S(2)}) %all-to-all-start.1) | async-done | bytes 262176 | tf_op jit(solution)/shard_map/all_to_all | solution.py:404
  114.2 0.3 reduce_sum.11
  114.5 0.2 broadcast_in_dim.16
  114.7 23.1 %all_to_all.16 = f32[256,1,384]{2,1,0:T(1,128)S(1)} all-to-all(f32[256,1,384]{2,1,0:T(1,128)S(1)} %broadcast_in_dim.16), channel_id=1, replica_groups=mesh['samples'=256] {'samples'}, dimensions={0} | all-to-all | bytes 786432 | tf_op jit(solution)/shard_map/all_to_all | solution.py:404
  137.8 9.0 %direction.1 = f32[3456]{0:T(1024)} custom-call(f32[256,384]{1,0:T(8,128)S(1)} %bitcast.8, bf16[256,3456]{1,0:T(8,128)(2,1)S(1)} %get-tuple-element.8.centered_ref), custom_call_target="tpu_custom_call" | custom-call | tf_op jit(solution)/shard_map/direction/pallas_call | solution.py:392
  (2 shorter events, 0.0 us)
Async XLA Ops:
  92.5 21.7 %all-to-all-start.1 = ((f32[256,1,256]{2,1,0:T(1,128)}), f32[256,1,256]{2,1,0:T(1,128)S(1)}, u32[]{:S(2)}, u32[]{:S(2)}) async-start(f32[256,1,256]{2,1,0:T(1,128)} %get-tuple-element.7), calls=%async_computation.1 | async-start | bytes 524288 | tf_op jit(solution)/shard_map/all_to_all | solution.py:404

commit v4 on v3

--- a/solution.py
+++ b/solution.py
@@ -323,7 +323,11 @@
     )(x)
 
 
-def direction_kernel(table_ref, centered_ref, out_ref, system, r_col, s_col):
+def spare_column(row):
+    return jnp.where(row < NS // 2, row + (NS // 2 - 1), row - NS // 2)
+
+
+def direction_kernel(table_ref, centered_ref, out_ref, system, gram_full, r_col, s_col):
     diagonal = lax.broadcasted_iota(jnp.int32, (NS, NS), 0) == lax.broadcasted_iota(
         jnp.int32, (NS, NS), 1
     )
@@ -337,8 +341,14 @@
     def as_row(values):
         return jnp.sum(jnp.where(diagonal, values, 0.0), axis=0, keepdims=True)
 
-    gram = table_ref[:, :NS]
-    energy = as_row(table_ref[:, NS : NS + 1])
+    row = lax.broadcasted_iota(jnp.int32, (NS, NS), 0)
+    column = lax.broadcasted_iota(jnp.int32, (NS, NS), 1)
+    table = table_ref[...]
+    spare = column == spare_column(row)
+    energy = as_row(total(jnp.where(spare, table, 0.0)))
+    mirrored = jnp.sum(jnp.where(row == spare_column(column), table, 0.0), axis=0, keepdims=True)
+    gram = jnp.where(spare, as_column(mirrored), table)
+    gram_full[...] = gram
     spread = (energy - total(energy) * (1.0 / NS)) * (1.0 / math.sqrt(NS))
     diag_term = SHIFT_RATIO * (total(as_row(gram)) * (1.0 / NS)) + 1e-06
     system[...] = gram + jnp.where(diagonal, diag_term, 0.0)
@@ -377,7 +387,7 @@
         iterate,
         (jnp.int32(0), zero, spread, zero, zero, jnp.full((1, 128), 1e30, F32), jnp.ones((1, 128), F32), start),
     )
-    square_total = total(coeffs * as_row(total(table_ref[:, :NS] * coeffs)))
+    square_total = total(coeffs * as_row(total(gram_full[...] * coeffs)))
     high = coeffs.astype(BF16).astype(F32)
     middle = (coeffs - high).astype(BF16).astype(F32)
     low = coeffs - high - middle
@@ -394,7 +404,7 @@
         out_shape=jax.ShapeDtypeStruct((OWN_ROWS * 128,), F32),
         in_specs=[vmem, vmem],
         out_specs=vmem,
-        scratch_shapes=[pltpu.VMEM((NS, NS), F32), pltpu.VMEM((NS, 128), F32), pltpu.VMEM((NS, 128), F32)],
+        scratch_shapes=[pltpu.VMEM((NS, NS), F32), pltpu.VMEM((NS, NS), F32), pltpu.VMEM((NS, 128), F32), pltpu.VMEM((NS, 128), F32)],
         compiler_params=pltpu.CompilerParams(vmem_limit_bytes=40 << 20),
         name="direction",
     )(table, centered)
@@ -408,8 +418,9 @@
     own = logderiv_rows(spin_configs, embedding, kernels, readout.reshape(1, CH))
     centered, part = partial_gram(exchange(own))
     gram_row = jnp.sum(exchange(part), axis=0)
-    line = jnp.concatenate([gram_row, jnp.broadcast_to(energy[:, None], (1, 128))], 1)
-    table = exchange(jnp.broadcast_to(line[None], (NS, 1, NS + 128))).reshape(NS, NS + 128)
+    at_spare = jnp.arange(NS) == spare_column(lax.axis_index("samples"))
+    line = jnp.where(at_spare, energy[0], gram_row)
+    table = exchange(jnp.broadcast_to(line[None], (NS, 1, NS))).reshape(NS, NS)
     return direction(table, centered)
 
 

time: 147 us -> 145 us (0.986)
  blocking collectives: 86.6 us -> 83.9 us
    all_to_all x2, blocking collectives: 86.6 us -> 83.9 us  [exchange(): lax.all_to_all(blocks, 'samples', split_axis=0, concat_axis=0, tiled=True)]
where the time goes in v4:
time: 145 us
  blocking collectives  83.9 us (58%)
  Pallas kernels  39.1 us (27%)
  waiting for transfers between devices  14.8 us (10%)
  starting transfers between devices  6.29 us (4%)
    all_to_all x2, blocking collectives, exchange(): lax.all_to_all(blocks, 'samples', split_axis=0, concat_axis=0, tiled=True)  83.9 us
    pallas_call x1, Pallas kernels, logderiv_rows(): pl.pallas_call(logderiv_kernel, out_shape=jax.ShapeDtypeStruct((NS, SEND_...  26.2 us
    all_to_all x1, waiting for transfers between devices, exchange(): lax.all_to_all(blocks, 'samples', split_axis=0, concat_axis=0, tiled=True)  14.8 us
    pallas_call x1, Pallas kernels, direction(): pl.pallas_call(direction_kernel, out_shape=jax.ShapeDtypeStruct((OWN_ROWS...  10.1 us
    all_to_all x1, starting transfers between devices, exchange(): lax.all_to_all(blocks, 'samples', split_axis=0, concat_axis=0, tiled=True)  6.29 us
  transfers between devices with their start and end apart: 1, of which 1 were waited for; matrix products, arithmetic and copies ran while one was open for 0% of the time, Pallas kernels for 0%

profile of v4, /device:TPU:1, one launch (start us, length us, event | category | flops | bytes accessed | tf_op | source)
XLA Modules:
  0.0 145.2 jit_solution(7369341937886852604)
XLA Ops:
  0.0 26.2 %logderiv.1 = s16[256,4,896]{2,1,0:T(4,128)(2,1)} custom-call(s32[1,256]{1,0:T(1,128)} %spin_ref.1, f32[9,64]{1,0:T(8,128)} %embed_ref.1, f32[1,64]{1,0:T(1,128)} %bitcast.9, f32[24,576,64]{2,1,0:T(8,128)} %bitcast.8), custom_call_target="tpu_custom_call" | custom-call | tf_op jit(solution)/shard_map/logderiv/pallas_call | solution.py:255
  26.2 63.5 %all_to_all.15.x_ref = s16[256,4,896]{2,1,0:T(4,128)(2,1)S(1)} all-to-all(s16[256,4,896]{2,1,0:T(4,128)(2,1)} %logderiv.1), channel_id=1, replica_groups=mesh['samples'=256] {'samples'}, dimensions={0} | all-to-all | bytes 3670016 | tf_op jit(solution)/shard_map/all_to_all | solution.py:414
  89.7 2.8 %partial_gram.1 = (bf16[256,3456]{1,0:T(8,128)(2,1)S(1)}, f32[256,1,256]{2,1,0:T(1,128)}) custom-call(s16[256,4,896]{2,1,0:T(4,128)(2,1)S(1)} %all_to_all.15.x_ref), custom_call_target="tpu_custom_call" | custom-call | tf_op jit(solution)/shard_map/partial_gram/pallas_call | solution.py:312
  92.5 6.3 %all-to-all-start.1 = ((f32[256,1,256]{2,1,0:T(1,128)}), f32[256,1,256]{2,1,0:T(1,128)S(1)}, u32[]{:S(2)}, u32[]{:S(2)}) async-start(f32[256,1,256]{2,1,0:T(1,128)} %get-tuple-element.7), calls=%async_computation.1 | async-start | bytes 524288 | tf_op jit(solution)/shard_map/all_to_all | solution.py:414
  99.4 14.8 %all-to-all-done.1 = f32[256,1,256]{2,1,0:T(1,128)S(1)} async-done(((f32[256,1,256]{2,1,0:T(1,128)}), f32[256,1,256]{2,1,0:T(1,128)S(1)}, u32[]{:S(2)}, u32[]{:S(2)}) %all-to-all-start.1) | async-done | bytes 262176 | tf_op jit(solution)/shard_map/all_to_all | solution.py:414
  114.2 0.3 reduce_sum.9
  114.5 0.1 broadcast_in_dim.13
  114.7 20.4 %all_to_all.16 = f32[256,1,256]{2,1,0:T(1,128)S(1)} all-to-all(f32[256,1,256]{2,1,0:T(1,128)S(1)} %broadcast_in_dim.13), channel_id=1, replica_groups=mesh['samples'=256] {'samples'}, dimensions={0} | all-to-all | bytes 524288 | tf_op jit(solution)/shard_map/all_to_all | solution.py:414
  135.1 10.1 %direction.1 = f32[3456]{0:T(1024)} custom-call(f32[256,256]{1,0:T(8,128)S(1)} %bitcast.7, bf16[256,3456]{1,0:T(8,128)(2,1)S(1)} %get-tuple-element.8.centered_ref), custom_call_target="tpu_custom_call" | custom-call | tf_op jit(solution)/shard_map/direction/pallas_call | solution.py:402
  (2 shorter events, 0.0 us)
Async XLA Ops:
  92.5 21.7 %all-to-all-start.1 = ((f32[256,1,256]{2,1,0:T(1,128)}), f32[256,1,256]{2,1,0:T(1,128)S(1)}, u32[]{:S(2)}, u32[]{:S(2)}) async-start(f32[256,1,256]{2,1,0:T(1,128)} %get-tuple-element.7), calls=%async_computation.1 | async-start | bytes 524288 | tf_op jit(solution)/shard_map/all_to_all | solution.py:414

commit v5 on v4

--- a/solution.py
+++ b/solution.py
@@ -180,7 +180,8 @@
             jnp.concatenate([group[i].T for group in groups], 0)
             for i in range(2)
         ]
-        sums = matmul(w_hi, u_hi[layer]) + (matmul(w_hi, u_lo[layer]) + matmul(w_lo, u_hi[layer]))
+        stacked = matmul(jnp.concatenate([w_hi, w_lo], 0), u_hi[layer])
+        sums = stacked[:WIDE] + (stacked[WIDE:] + matmul(w_hi, u_lo[layer]))
         moved = [column_roll(sums[CH * i : CH * i + CH], step, place) for i, step in enumerate(STEPS)]
         return hidden + (moved[0] + moved[1] + moved[2])
 
@@ -225,7 +226,8 @@
             )
             for part in split_two(weights[layer])
         ]
-        sums = matmul(w_hi, g_hi) + (matmul(w_hi, g_lo) + matmul(w_lo, g_hi))
+        stacked = matmul(jnp.concatenate([w_hi, w_lo], 0), g_hi)
+        sums = stacked[:WIDE] + (stacked[WIDE:] + matmul(w_hi, g_lo))
         x_hi, x_lo = [jnp.concatenate([part, part[128:]], 0) for part in (g_hi, g_lo)]
         both = matmul_nt(jnp.concatenate([u_hi[layer], u_lo[layer]], 0), x_hi)
         products = both[:WIDE] + (both[WIDE:] + matmul_nt(u_hi[layer], x_lo))
@@ -359,7 +361,7 @@
 
     def iterate(state):
         count, x, r, p, s, last, alpha, _ = state
-        for _ in range(4):
+        for _ in range(6):
             w_col = total(system[...] * r)
             r_all = r_col[...]
             norm = jnp.sum(r_all * r_all, axis=0, keepdims=True)

time: 145 us -> 144 us (level)
  no operation moved by 1% of the time
where the time goes in v5:
time: 144 us
  blocking collectives  83.9 us (58%)
  Pallas kernels  37.9 us (26%)
  waiting for transfers between devices  14.8 us (10%)
  starting transfers between devices  6.29 us (4%)
    all_to_all x2, blocking collectives, exchange(): lax.all_to_all(blocks, 'samples', split_axis=0, concat_axis=0, tiled=True)  83.9 us
    pallas_call x1, Pallas kernels, logderiv_rows(): pl.pallas_call(logderiv_kernel, out_shape=jax.ShapeDtypeStruct((NS, SEND_...  26 us
    all_to_all x1, waiting for transfers between devices, exchange(): lax.all_to_all(blocks, 'samples', split_axis=0, concat_axis=0, tiled=True)  14.8 us
    pallas_call x1, Pallas kernels, direction(): pl.pallas_call(direction_kernel, out_shape=jax.ShapeDtypeStruct((OWN_ROWS...  9.06 us
    all_to_all x1, starting transfers between devices, exchange(): lax.all_to_all(blocks, 'samples', split_axis=0, concat_axis=0, tiled=True)  6.29 us
  transfers between devices with their start and end apart: 1, of which 1 were waited for; matrix products, arithmetic and copies ran while one was open for 0% of the time, Pallas kernels for 0%

profile of v5, /device:TPU:1, one launch (start us, length us, event | category | flops | bytes accessed | tf_op | source)
XLA Modules:
  0.0 144.0 jit_solution(12931712640478762663)
XLA Ops:
  0.0 26.0 %logderiv.1 = s16[256,4,896]{2,1,0:T(4,128)(2,1)} custom-call(s32[1,256]{1,0:T(1,128)} %spin_ref.1, f32[9,64]{1,0:T(8,128)} %embed_ref.1, f32[1,64]{1,0:T(1,128)} %bitcast.9, f32[24,576,64]{2,1,0:T(8,128)} %bitcast.8), custom_call_target="tpu_custom_call" | custom-call | tf_op jit(solution)/shard_map/logderiv/pallas_call | solution.py:257
  26.0 63.5 %all_to_all.15.x_ref = s16[256,4,896]{2,1,0:T(4,128)(2,1)S(1)} all-to-all(s16[256,4,896]{2,1,0:T(4,128)(2,1)} %logderiv.1), channel_id=1, replica_groups=mesh['samples'=256] {'samples'}, dimensions={0} | all-to-all | bytes 3670016 | tf_op jit(solution)/shard_map/all_to_all | solution.py:416
  89.5 2.8 %partial_gram.1 = (bf16[256,3456]{1,0:T(8,128)(2,1)S(1)}, f32[256,1,256]{2,1,0:T(1,128)}) custom-call(s16[256,4,896]{2,1,0:T(4,128)(2,1)S(1)} %all_to_all.15.x_ref), custom_call_target="tpu_custom_call" | custom-call | tf_op jit(solution)/shard_map/partial_gram/pallas_call | solution.py:314
  92.3 6.3 %all-to-all-start.1 = ((f32[256,1,256]{2,1,0:T(1,128)}), f32[256,1,256]{2,1,0:T(1,128)S(1)}, u32[]{:S(2)}, u32[]{:S(2)}) async-start(f32[256,1,256]{2,1,0:T(1,128)} %get-tuple-element.7), calls=%async_computation.1 | async-start | bytes 524288 | tf_op jit(solution)/shard_map/all_to_all | solution.py:416
  99.3 14.8 %all-to-all-done.1 = f32[256,1,256]{2,1,0:T(1,128)S(1)} async-done(((f32[256,1,256]{2,1,0:T(1,128)}), f32[256,1,256]{2,1,0:T(1,128)S(1)}, u32[]{:S(2)}, u32[]{:S(2)}) %all-to-all-start.1) | async-done | bytes 262176 | tf_op jit(solution)/shard_map/all_to_all | solution.py:416
  114.1 0.3 reduce_sum.9
  114.4 0.1 broadcast_in_dim.13
  114.5 20.4 %all_to_all.16 = f32[256,1,256]{2,1,0:T(1,128)S(1)} all-to-all(f32[256,1,256]{2,1,0:T(1,128)S(1)} %broadcast_in_dim.13), channel_id=1, replica_groups=mesh['samples'=256] {'samples'}, dimensions={0} | all-to-all | bytes 524288 | tf_op jit(solution)/shard_map/all_to_all | solution.py:416
  135.0 9.1 %direction.1 = f32[3456]{0:T(1024)} custom-call(f32[256,256]{1,0:T(8,128)S(1)} %bitcast.7, bf16[256,3456]{1,0:T(8,128)(2,1)S(1)} %get-tuple-element.8.centered_ref), custom_call_target="tpu_custom_call" | custom-call | tf_op jit(solution)/shard_map/direction/pallas_call | solution.py:404
  (2 shorter events, 0.0 us)
Async XLA Ops:
  92.3 21.7 %all-to-all-start.1 = ((f32[256,1,256]{2,1,0:T(1,128)}), f32[256,1,256]{2,1,0:T(1,128)S(1)}, u32[]{:S(2)}, u32[]{:S(2)}) async-start(f32[256,1,256]{2,1,0:T(1,128)} %get-tuple-element.7), calls=%async_computation.1 | async-start | bytes 524288 | tf_op jit(solution)/shard_map/all_to_all | solution.py:416
